TPU v7x, 512 devices: a whole 4x8x8 slice. The times are simulated.
512 devices in a mesh: box: 128 (over z, y, core), coarse: 4 (over x).
Axes of the slice: x: 4, y: 8, z: 8, core: 2. Of those that a mesh axis runs over, the one named last changes fastest.
Arguments:
- points: float32 [128, 8, 3, 256], P('box', 'coarse'), may hold values from 0 to 1
- self_gain: float32 [128, 8, 256], P('box', 'coarse'), may hold values from 1.5 to 4
- pivots: int32 [128, 8, 256], P('box', 'coarse'), may hold values from 0 to 255, each once within a row
- interp: float32 [128, 8, 128, 128], P('box', 'coarse'), may hold values from -0.5 to 0.5
- neighbors: int32 [128, 8, 6], P('box', 'coarse'), may hold values from 0 to 15, as said below
- rhs: float32 [128, 8, 256, 512], P('box', 'coarse'), may hold values from -6 to 6
Outputs:
- solution: float32 [128, 8, 256, 512], P('box', 'coarse')
Inputs may be any that keep to these rules, and one draw needn't show every extreme that they name: `pivots`: each box's row orders all 256 of its points once; the first 128 form its skeleton. `neighbors`: each box lists 6 different boxes; n < 8 names child n of the previous parent, 8 + n child n of the next parent.
All inputs are finite; a program needn't handle non-finite values.
Results may differ from a plain program's by a relative error of at most 0.0003.
Values sent between devices are 32-bit elements; how exact they have to be, the bound alone decides.
No kernel may reach another device: no remote copies, remote signals or barrier semaphores. Data moves between devices by JAX's collectives and lax.ppermute only.
A program may use at most 64 MiB of HBM per device.

v0:
```python
import jax
import jax.numpy as jnp
from jax import lax
from jax.sharding import PartitionSpec as P

NP = 256
CHILD = 8
softening = 0.0025


def shifted_2(block, axis, distance):
    devices = range(lax.axis_size(axis))
    route = [(i - distance, i) for i in devices if i - distance in devices]
    return lax.ppermute(block, axis, route)


def kernel_block(targets, sources):
    difference = targets[:, :, None] - sources[:, None, :]
    return lax.rsqrt(jnp.sum(difference * difference, axis=0) + softening)


def product(left, right):
    return jnp.dot(left, right, precision=lax.Precision.HIGHEST)


def chol_apply(factor, right):
    return jax.scipy.linalg.cho_solve((factor, True), right)


def box_corners(group_ids, child_ids):
    along_x = 2 * group_ids + child_ids % 2
    along_y = child_ids // 2 % 2
    along_z = child_ids // 4
    return jnp.stack([along_x, along_y, along_z], axis=-1).astype(jnp.float32)


def factor_box(located, gains, order, interp, right_side):
    ordered = jnp.take(located, order, axis=1)
    ordered_gain = jnp.take(gains, order, axis=0)
    ordered_rhs = jnp.take(right_side, order, axis=0)
    kernel = kernel_block(ordered, ordered)
    count = ordered.shape[1]
    rank = interp.shape[0]
    matrix = (kernel + jnp.diag(ordered_gain * jnp.sum(kernel, axis=1))) / count
    skel_skel = matrix[:rank, :rank]
    skel_red = matrix[:rank, rank:]
    red_skel = matrix[rank:, :rank]
    red_red = matrix[rank:, rank:]
    shifted = product(interp.T, skel_skel)
    red_block = (
        red_red - product(interp.T, skel_red) - product(red_skel, interp) + product(shifted, interp)
    )
    cross = red_skel - shifted
    red_factor = jnp.linalg.cholesky(red_block)
    coupling = chol_apply(red_factor, cross)
    schur = skel_skel - product(cross.T, coupling)
    reduced = ordered_rhs[rank:] - product(interp.T, ordered_rhs[:rank])
    interior = chol_apply(red_factor, reduced)
    skeleton_rhs = ordered_rhs[:rank] - product(coupling.T, reduced)
    schur_factor = jnp.linalg.cholesky(schur)
    local_solve = chol_apply(schur_factor, skeleton_rhs)
    return (schur_factor, coupling, interior, local_solve, ordered[:, :rank])


def coarse_weights(neighbor_rows, own_child):
    listed = jnp.any(
        neighbor_rows[:, :, None] == jnp.arange(2 * CHILD, dtype=jnp.int32)[None, None, :], axis=1
    ).astype(jnp.float32)
    siblings = (own_child[:, None] != jnp.arange(CHILD, dtype=jnp.int32)[None, :]).astype(
        jnp.float32
    )
    return jnp.concatenate([listed[:, :CHILD], siblings, listed[:, CHILD:]], axis=1)


def coarse_terms(skeleton, cand_pts, cand_rhs, weights):
    blocks = jax.vmap(
        lambda target: jax.vmap(lambda source: kernel_block(target, source))(cand_pts)
    )(skeleton)
    return (
        jnp.einsum(
            "bckl,cln->bkn",
            blocks * weights[:, :, None, None],
            cand_rhs,
            precision=lax.Precision.HIGHEST,
        )
        / NP
    )


def finish_box(schur_factor, coupling, interior, local_solve, correction, interp, order):
    coarse = local_solve - chol_apply(schur_factor, correction)
    redundant = interior - product(coupling, coarse)
    skeletal = coarse - product(interp, redundant)
    ordered = jnp.concatenate([skeletal, redundant], axis=0)
    return jnp.zeros_like(ordered).at[order].set(ordered)


def per_device(points, self_gain, pivots, interp, neighbors, rhs):
    groups_here = points.shape[0]
    children_here = points.shape[1]
    group_ids = lax.axis_index("box") * groups_here + jnp.arange(groups_here, dtype=jnp.int32)
    child_ids = lax.axis_index("coarse") * children_here + jnp.arange(
        children_here, dtype=jnp.int32
    )
    zero_grid = jnp.zeros((groups_here, children_here), jnp.int32)
    located = points + box_corners(group_ids[:, None] + zero_grid, child_ids[None, :])[..., None]
    schur_factor, coupling, interior, local_solve, skeleton = jax.vmap(jax.vmap(factor_box))(
        located, self_gain, pivots, interp, rhs
    )
    full_rhs, full_pts = (
        lax.all_gather(local_solve, "coarse", axis=1, tiled=True),
        lax.all_gather(skeleton, "coarse", axis=1, tiled=True),
    )
    left_rhs, left_pts = shifted_2((full_rhs, full_pts), "box", 1)
    right_rhs, right_pts = shifted_2((full_rhs, full_pts), "box", -1)
    wide_rhs = jnp.concatenate([left_rhs, full_rhs, right_rhs], axis=0)
    wide_pts = jnp.concatenate([left_pts, full_pts, right_pts], axis=0)
    cand_rhs = jnp.concatenate([wide_rhs[:-2], wide_rhs[1:-1], wide_rhs[2:]], axis=1)
    cand_pts = jnp.concatenate([wide_pts[:-2], wide_pts[1:-1], wide_pts[2:]], axis=1)
    weights = jax.vmap(coarse_weights, in_axes=(0, None))(neighbors, child_ids)
    correction = jax.vmap(coarse_terms)(skeleton, cand_pts, cand_rhs, weights)
    return jax.vmap(jax.vmap(finish_box))(
        schur_factor, coupling, interior, local_solve, correction, interp, pivots
    )


def solution(mesh):
    in_specs = (
        P("box", "coarse", None, None),
        P("box", "coarse", None),
        P("box", "coarse", None),
        P("box", "coarse", None, None),
        P("box", "coarse", None),
        P("box", "coarse", None, None),
    )
    out_specs = P("box", "coarse", None, None)
    return jax.shard_map(
        per_device, mesh=mesh, in_specs=in_specs, out_specs=out_specs, check_vma=False
    )
```

profile of v0, /device:TPU:25, one launch (start us, length us, event | category | flops | bytes accessed | tf_op | source)
XLA Modules:
  0.0 234.6 jit_solution(4038636412961429317)
XLA Ops:
  6.6 0.8 fusion.71
  7.3 0.7 fusion.74
  8.3 0.8 broadcast_add_fusion
  9.3 3.6 %gather_fusion = f32[512,3]{1,0:T(8,128)S(1)} fusion(f32[1,2,3,256]{2,3,1,0:T(8,128)S(1)} %copy.111, s32[512]{0:T(512)S(1)} %bitcast.209), kind=kCustom, calls=%fused_computation | custom fusion | bytes 18432 | tf_op jit(solution)/shard_map/vmap(vmap(jit(_take)))/gather | solution.py:38
  13.7 4.7 %gather_fusion.1 = f32[512]{0:T(512)S(1)} fusion(f32[1,2,256]{2,1,0:T(2,128)S(1)} %copy-done.1, s32[512]{0:T(512)S(1)} %bitcast.210), kind=kCustom, calls=%fused_computation.1 | custom fusion | bytes 10240 | tf_op jit(solution)/shard_map/vmap(vmap(jit(_take)))/gather | solution.py:39
  20.0 23.5 %custom-call.27 = f32[1,2,128,128]{3,2,1,0:T(8,128)S(1)} custom-call(f32[1,2,128,128]{3,2,1,0:T(8,128)S(1)} %fusion.49), custom_call_target="Cholesky" | custom-call | tf_op jit(solution)/shard_map/vmap(vmap(jit(cholesky)))/cholesky | solution.py:54
  43.7 19.7 %custom-call.15 = f32[1,2,1,128,128]{3,4,2,1,0:T(8,128)S(1)} custom-call(f32[1,2,1,128,128]{4,3,2,1,0:T(8,128)S(1)} %fusion.59), custom_call_target="InvertDiagBlocksLowerTriangular" | custom-call | tf_op jit(solution)/shard_map/vmap(vmap(jit(_cho_solve)))/triangular_solve | solution.py:27
  64.6 23.6 %custom-call.28 = f32[1,2,128,128]{3,2,1,0:T(8,128)S(1)} custom-call(f32[1,2,128,128]{3,2,1,0:T(8,128)S(1)} %fusion.41), custom_call_target="Cholesky" | custom-call | tf_op jit(solution)/shard_map/vmap(vmap(jit(cholesky)))/cholesky | solution.py:60
  88.5 19.7 %custom-call.29 = f32[1,2,1,128,128]{3,4,2,1,0:T(8,128)S(1)} custom-call(f32[1,2,1,128,128]{4,3,2,1,0:T(8,128)S(1)} %select_bitcast_fusion), custom_call_target="InvertDiagBlocksLowerTriangular" | custom-call | tf_op jit(solution)/shard_map/vmap(vmap(jit(_cho_solve)))/triangular_solve | solution.py:27
  108.2 3.9 %gather_fusion.2 = f32[512,512]{1,0:T(8,128)S(1)} fusion(f32[1,2,256,512]{3,2,1,0:T(8,128)S(1)} %copy-done, s32[512]{0:T(512)S(1)} %bitcast.211), kind=kCustom, calls=%fused_computation.2 | custom fusion | bytes 2103296 | tf_op jit(solution)/shard_map/vmap(vmap(jit(_take)))/gather | solution.py:40
  112.6 0.6 fusion.17
  113.4 0.6 fusion.19
  114.0 0.6 fusion.39
  114.6 1.4 fusion.37
  116.0 40.4 %all-gather.2.cloned.1.call-done = f32[1,8,128,512]{3,2,0,1:T(8,128)} async-done(((f32[1,2,128,512]{3,2,0,1:T(8,128)}), f32[1,8,128,512]{3,2,0,1:T(8,128)}) %all-gather.2.cloned.1.call-update) | async-done | bytes 2097168 | tf_op jit(solution)/shard_map/all_gather | solution.py:111
  156.5 5.2 %collective-permute-start.2 = (f32[1,8,128,512]{3,2,1,0:T(8,128)}, f32[1,8,128,512]{3,2,1,0:T(8,128)S(1)}, u32[]{:S(2)}, u32[]{:S(2)}) collective-permute-start(f32[1,8,128,512]{3,2,1,0:T(8,128)} %bitcast.219), channel_id=1, source_target_pairs={{0,4},{4,8},{8,12},{12,16},{16,20},{20,24},{24,28},{28,32},{32,36}... | collective-permute-start | bytes 6291464 | tf_op jit(solution)/shard_map/ppermute | solution.py:14
  161.7 1.9 collective-permute-start.3
  163.6 9.0 %all_gather.6 = f32[1,8,3,128]{3,0,2,1:T(1,128)S(1)} all-gather(f32[1,2,3,128]{3,0,2,1:T(1,128)S(1)} %copy.134), channel_id=1, replica_groups=mesh['box'=128,'coarse'=4] {'coarse'}, dimensions={1}, use_global_device_ids=true | all-gather | bytes 15360 | tf_op jit(solution)/shard_map/all_gather | solution.py:112
  172.7 7.7 %collective-permute-start = (f32[1,8,3,128]{3,0,2,1:T(1,128)S(1)}, f32[1,8,3,128]{3,0,2,1:T(1,128)S(1)}, u32[]{:S(2)}, u32[]{:S(2)}) collective-permute-start(f32[1,8,3,128]{3,0,2,1:T(1,128)S(1)} %all_gather.6), channel_id=1, source_target_pairs={{0,4},{4,8},{8,12},{12,16},{16,20},{20,24},{24,28},{28,32},{32,36}... | collective-permute-start | bytes 36872 | tf_op jit(solution)/shard_map/ppermute | solution.py:14
  180.4 2.1 collective-permute-start.1
  182.8 0.6 fusion.43
  183.6 1.4 collective-permute-done
  185.0 5.6 %collective-permute-done.1 = f32[1,8,3,128]{3,0,2,1:T(1,128)S(1)} collective-permute-done((f32[1,8,3,128]{3,0,2,1:T(1,128)S(1)}, f32[1,8,3,128]{3,0,2,1:T(1,128)S(1)}, u32[]{:S(2)}, u32[]{:S(2)}) %collective-permute-start.1) | collective-permute-done | bytes 12320 | tf_op jit(solution)/shard_map/ppermute | solution.py:14
  190.6 1.2 multiply_reduce_fusion
  191.8 5.7 %fusion.13 = f32[2,128,512]{2,1,0:T(8,128)S(1)} fusion(f32[1,8,128,512]{3,2,1,0:T(8,128)S(1)} %collective-permute-done.3, f32[1,8,128,512]{3,2,1,0:T(8,128)S(1)} %bitcast.221, f32[1,8,128,512]{3,2,1,0:T(8,128)S(1)} %collective-permute-done.2, f32[2,24,128,128]{3,2,1,0:T(8,128)S(1)} %multiply_reduce_fusion, f32[2,24]{1,0:T(2,128)S(1)} %maximum_bitcast_fusion.7), kind=kOutput, calls=%fused_computation.24 | convolution fusion | flops 4836687872 | bytes 9961664 | tf_op jit(solution)/shard_map/vmap(bckl,cln->bkn)/dot_general | solution.py:80
  197.5 0.6 fusion.35
  198.1 0.6 fusion.20
  198.7 0.6 convolution_bitcast_fusion.1
  199.3 0.6 fusion.21
  199.9 0.6 fusion.22
  200.7 26.0 %scatter_fusion = f32[2,256,512]{2,1,0:T(8,128)S(1)} fusion(f32[2,256,512]{2,1,0:T(8,128)S(1)} %broadcast.679, s32[512]{0:T(512)S(1)} %bitcast.212, f32[512,512]{1,0:T(8,128)S(1)} %bitcast.214), kind=kCustom, calls=%fused_computation.3 | custom fusion | bytes 3149824 | tf_op jit(solution)/shard_map/vmap(vmap())/scatter | solution.py:95
  226.8 1.0 copy-done.2
  (83 shorter events, 5.7 us)
Async XLA Ops:
  6.5 101.7 %copy-start = (f32[1,2,256,512]{3,2,1,0:T(8,128)S(1)}, f32[1,2,256,512]{3,2,1,0:T(8,128)}, u32[]{:S(2)}) copy-start(f32[1,2,256,512]{3,2,1,0:T(8,128)} %param.14) | copy-start | bytes 3145732
  6.5 11.8 %copy-start.7 = (s32[1,2,256]{2,1,0:T(2,128)S(1)}, s32[1,2,256]{2,1,0:T(2,128)}, u32[]{:S(2)}) copy-start(s32[1,2,256]{2,1,0:T(2,128)} %param.11) | copy-start | bytes 6148
  6.5 7.1 %copy-start.1 = (f32[1,2,256]{2,1,0:T(2,128)S(1)}, f32[1,2,256]{2,1,0:T(2,128)}, u32[]{:S(2)}) copy-start(f32[1,2,256]{2,1,0:T(2,128)} %param.10) | copy-start | bytes 6148
  6.5 150.0 %all-gather.2.cloned.1.call-start = ((), (), s32[]{:S(2)}) async-start(), calls=%async_computation | async-start | bytes 2621440 | tf_op jit(solution)/shard_map/all_gather | solution.py:111
  9.2 9.3 %copy-start.4 = (f32[1,2,128,128]{3,2,1,0:T(8,128)S(1)}, f32[1,2,128,128]{3,2,1,0:T(8,128)}, u32[]{:S(2)}) copy-start(f32[1,2,128,128]{3,2,1,0:T(8,128)} %param.12) | copy-start | bytes 393220
  64.1 24.4 %copy-start.5 = (f32[2,128,128]{2,1,0:T(8,128)}, f32[2,128,128]{2,1,0:T(8,128)S(1)}, u32[]{:S(2)}) copy-start(f32[2,128,128]{2,1,0:T(8,128)S(1)} %fusion.45) | copy-start | bytes 393220
  112.5 0.9 copy-start.6
  112.6 70.0 %copy-start.9 = (s32[1,2,6]{2,1,0:T(2,128)S(1)}, s32[1,2,6]{2,1,0:T(2,128)}, u32[]{:S(2)}) copy-start(s32[1,2,6]{2,1,0:T(2,128)} %param.13) | copy-start | bytes 148
  156.5 35.3 %copy-start.8 = (f32[1,8,128,512]{3,2,0,1:T(8,128)S(1)}, f32[1,8,128,512]{3,2,0,1:T(8,128)}, u32[]{:S(2)}) copy-start(f32[1,8,128,512]{3,2,0,1:T(8,128)} %all-gather.2.cloned.1.call-done) | copy-start | bytes 6291460
  156.5 35.3 %collective-permute-start.2 = (f32[1,8,128,512]{3,2,1,0:T(8,128)}, f32[1,8,128,512]{3,2,1,0:T(8,128)S(1)}, u32[]{:S(2)}, u32[]{:S(2)}) collective-permute-start(f32[1,8,128,512]{3,2,1,0:T(8,128)} %bitcast.219), channel_id=1, source_target_pairs={{0,4},{4,8},{8,12},{12,16},{16,20},{20,24},{24,28},{28,32},{32,36}... | collective-permute-start | bytes 6291464 | tf_op jit(solution)/shard_map/ppermute | solution.py:14
  161.7 30.1 %collective-permute-start.3 = (f32[1,8,128,512]{3,2,1,0:T(8,128)}, f32[1,8,128,512]{3,2,1,0:T(8,128)S(1)}, u32[]{:S(2)}, u32[]{:S(2)}) collective-permute-start(f32[1,8,128,512]{3,2,1,0:T(8,128)} %bitcast.220), channel_id=1, source_target_pairs={{4,0},{8,4},{12,8},{16,12},{20,16},{24,20},{28,24},{32,28},{36,32}... | collective-permute-start | bytes 6291464 | tf_op jit(solution)/shard_map/ppermute | solution.py:14
  172.7 12.3 %collective-permute-start = (f32[1,8,3,128]{3,0,2,1:T(1,128)S(1)}, f32[1,8,3,128]{3,0,2,1:T(1,128)S(1)}, u32[]{:S(2)}, u32[]{:S(2)}) collective-permute-start(f32[1,8,3,128]{3,0,2,1:T(1,128)S(1)} %all_gather.6), channel_id=1, source_target_pairs={{0,4},{4,8},{8,12},{12,16},{16,20},{20,24},{24,28},{28,32},{32,36}... | collective-permute-start | bytes 36872 | tf_op jit(solution)/shard_map/ppermute | solution.py:14
  180.4 10.2 %collective-permute-start.1 = (f32[1,8,3,128]{3,0,2,1:T(1,128)S(1)}, f32[1,8,3,128]{3,0,2,1:T(1,128)S(1)}, u32[]{:S(2)}, u32[]{:S(2)}) collective-permute-start(f32[1,8,3,128]{3,0,2,1:T(1,128)S(1)} %all_gather.6), channel_id=1, source_target_pairs={{4,0},{8,4},{12,8},{16,12},{20,16},{24,20},{28,24},{32,28},{36,32}... | collective-permute-start | bytes 36872 | tf_op jit(solution)/shard_map/ppermute | solution.py:14
  191.8 6.4 %copy-start.3 = (f32[2,128,512]{2,1,0:T(8,128)S(1)}, f32[2,128,512]{2,1,0:T(8,128)}, u32[]{:S(2)}) copy-start(f32[2,128,512]{2,1,0:T(8,128)} %fusion.37) | copy-start | bytes 1572868
  226.8 1.0 copy-start.2
Sparse Core Ops, SparseCore 0:
  116.2 40.2 all-gather.1
where the time goes:
time: 235 us
  other arithmetic  91.5 us (39%)
  waiting for transfers between devices  47.5 us (20%)
  local copies, waits for them, and re-layouts  40.7 us (17%)
  starting transfers between devices  17 us (7%)
  matrix products  14.8 us (6%)
  between operations  14 us (6%)
  blocking collectives  9.05 us (4%)
    all_gather x1, waiting for transfers between devices, per_device(): lax.all_gather(local_solve, 'coarse', axis=1, tiled=True)  40.4 us
    another operation x5, other arithmetic, chol_apply(): return jax.scipy.linalg.cho_solve((factor, True), right)  39.6 us
    scatter x2, local copies, waits for them, and re-layouts, finish_box(): return jnp.zeros_like(ordered).at[order].set(ordered)  26 us
    another operation x4, other arithmetic, factor_box(): schur_factor = jnp.linalg.cholesky(schur)  23.8 us
    another operation x3, other arithmetic, factor_box(): red_factor = jnp.linalg.cholesky(red_block)  23.6 us
    ppermute x4, starting transfers between devices, shifted_2(): return lax.ppermute(block, axis, route)  17 us
    all_gather x1, blocking collectives, per_device(): lax.all_gather(skeleton, 'coarse', axis=1, tiled=True)  9.05 us
    ppermute x4, waiting for transfers between devices, shifted_2(): return lax.ppermute(block, axis, route)  7.02 us
  transfers between devices with their start and end apart: 5, of which 3 were waited for; matrix products, arithmetic and copies ran while one was open for 1% of the time, Pallas kernels for 0%

commit v1 on v0

--- a/solution.py
+++ b/solution.py
@@ -6,6 +6,11 @@
 NP = 256
 CHILD = 8
 softening = 0.0025
+
+
+def all_by_exchange(value, axis, dim):
+    sent = jnp.stack([value] * lax.axis_size(axis))
+    return jnp.concatenate(lax.all_to_all(sent, axis, 0, 0), axis=dim)
 
 
 def shifted_2(block, axis, distance):
@@ -108,7 +113,7 @@
         located, self_gain, pivots, interp, rhs
     )
     full_rhs, full_pts = (
-        lax.all_gather(local_solve, "coarse", axis=1, tiled=True),
+        all_by_exchange(local_solve, "coarse", 1),
         lax.all_gather(skeleton, "coarse", axis=1, tiled=True),
     )
     left_rhs, left_pts = shifted_2((full_rhs, full_pts), "box", 1)

time: 235 us -> 216 us (0.919)
  the two profiles are of different devices: /device:TPU:25 before, /device:TPU:249 now
where the time goes in v1:
time: 216 us
  other arithmetic  91.5 us (42%)
  local copies, waits for them, and re-layouts  42.3 us (20%)
  waiting for transfers between devices  32.8 us (15%)
  starting transfers between devices  24.2 us (11%)
  matrix products  15.6 us (7%)
  blocking collectives  9.05 us (4%)
    another operation x5, other arithmetic, chol_apply(): return jax.scipy.linalg.cho_solve((factor, True), right)  39.6 us
    scatter x2, local copies, waits for them, and re-layouts, finish_box(): return jnp.zeros_like(ordered).at[order].set(ordered)  26 us
    all_to_all x1, waiting for transfers between devices, all_by_exchange(): return jnp.concatenate(lax.all_to_all(sent, axis, 0, 0), axis=dim)  25.8 us
    another operation x4, other arithmetic, factor_box(): schur_factor = jnp.linalg.cholesky(schur)  23.8 us
    another operation x3, other arithmetic, factor_box(): red_factor = jnp.linalg.cholesky(red_block)  23.6 us
    ppermute x4, starting transfers between devices, shifted_2(): return lax.ppermute(block, axis, route)  19.7 us
    all_gather x1, blocking collectives, per_device(): lax.all_gather(skeleton, 'coarse', axis=1, tiled=True)  9.05 us
    dot_general x1, matrix products, coarse_terms(): jnp.einsum('bckl,cln->bkn', blocks * weights[:, :, None, None], cand_rhs,...  7.26 us
  transfers between devices with their start and end apart: 5, of which 2 were waited for; matrix products, arithmetic and copies ran while one was open for 1% of the time, Pallas kernels for 0%

profile of v1, /device:TPU:249, one launch (start us, length us, event | category | flops | bytes accessed | tf_op | source)
XLA Modules:
  0.0 216.1 jit_solution(12918264524999419002)
XLA Ops:
  0.0 0.8 fusion.71
  0.8 0.7 fusion.74
  1.7 0.8 broadcast_add_fusion
  2.8 3.6 %gather_fusion = f32[512,3]{1,0:T(8,128)S(1)} fusion(f32[1,2,3,256]{2,3,1,0:T(8,128)S(1)} %copy.103, s32[512]{0:T(512)S(1)} %bitcast.205), kind=kCustom, calls=%fused_computation | custom fusion | bytes 18432 | tf_op jit(solution)/shard_map/vmap(vmap(jit(_take)))/gather | solution.py:43
  7.1 4.7 %gather_fusion.1 = f32[512]{0:T(512)S(1)} fusion(f32[1,2,256]{2,1,0:T(2,128)S(1)} %copy-done.1, s32[512]{0:T(512)S(1)} %bitcast.206), kind=kCustom, calls=%fused_computation.1 | custom fusion | bytes 10240 | tf_op jit(solution)/shard_map/vmap(vmap(jit(_take)))/gather | solution.py:44
  13.5 23.5 %custom-call.27 = f32[1,2,128,128]{3,2,1,0:T(8,128)S(1)} custom-call(f32[1,2,128,128]{3,2,1,0:T(8,128)S(1)} %fusion.49), custom_call_target="Cholesky" | custom-call | tf_op jit(solution)/shard_map/vmap(vmap(jit(cholesky)))/cholesky | solution.py:59
  37.2 19.7 %custom-call.15 = f32[1,2,1,128,128]{3,4,2,1,0:T(8,128)S(1)} custom-call(f32[1,2,1,128,128]{4,3,2,1,0:T(8,128)S(1)} %fusion.59), custom_call_target="InvertDiagBlocksLowerTriangular" | custom-call | tf_op jit(solution)/shard_map/vmap(vmap(jit(_cho_solve)))/triangular_solve | solution.py:32
  58.1 23.6 %custom-call.28 = f32[1,2,128,128]{3,2,1,0:T(8,128)S(1)} custom-call(f32[1,2,128,128]{3,2,1,0:T(8,128)S(1)} %fusion.41), custom_call_target="Cholesky" | custom-call | tf_op jit(solution)/shard_map/vmap(vmap(jit(cholesky)))/cholesky | solution.py:65
  82.0 19.7 %custom-call.29 = f32[1,2,1,128,128]{3,4,2,1,0:T(8,128)S(1)} custom-call(f32[1,2,1,128,128]{4,3,2,1,0:T(8,128)S(1)} %select_bitcast_fusion), custom_call_target="InvertDiagBlocksLowerTriangular" | custom-call | tf_op jit(solution)/shard_map/vmap(vmap(jit(_cho_solve)))/triangular_solve | solution.py:32
  101.7 3.9 %gather_fusion.2 = f32[512,512]{1,0:T(8,128)S(1)} fusion(f32[1,2,256,512]{3,2,1,0:T(8,128)S(1)} %copy-done, s32[512]{0:T(512)S(1)} %bitcast.207), kind=kCustom, calls=%fused_computation.2 | custom fusion | bytes 2103296 | tf_op jit(solution)/shard_map/vmap(vmap(jit(_take)))/gather | solution.py:45
  106.1 0.6 fusion.17
  107.4 0.6 fusion.39
  108.1 0.6 fusion.37
  108.7 1.6 stack.5
  110.3 4.4 %all-to-all-start = ((f32[4,1,2,128,512]{4,3,2,1,0:T(8,128)}), f32[4,1,2,128,512]{4,3,2,1,0:T(8,128)}, u32[]{:S(2)}, u32[]{:S(2)}) async-start(f32[4,1,2,128,512]{4,3,2,1,0:T(8,128)} %stack.5), calls=%async_computation | async-start | bytes 4194304 | tf_op jit(solution)/shard_map/all_to_all | solution.py:13
  114.7 25.8 %all-to-all-done = f32[4,1,2,128,512]{4,3,2,1,0:T(8,128)} async-done(((f32[4,1,2,128,512]{4,3,2,1,0:T(8,128)}), f32[4,1,2,128,512]{4,3,2,1,0:T(8,128)}, u32[]{:S(2)}, u32[]{:S(2)}) %all-to-all-start) | async-done | bytes 2097184 | tf_op jit(solution)/shard_map/all_to_all | solution.py:13
  140.5 5.8 %collective-permute-start.2 = (f32[1,8,128,512]{3,2,1,0:T(8,128)}, f32[1,8,128,512]{3,2,1,0:T(8,128)S(1)}, u32[]{:S(2)}, u32[]{:S(2)}) collective-permute-start(f32[1,8,128,512]{3,2,1,0:T(8,128)} %bitcast.44), channel_id=1, source_target_pairs={{0,4},{4,8},{8,12},{12,16},{16,20},{20,24},{24,28},{28,32},{32,36}... | collective-permute-start | bytes 6291464 | tf_op jit(solution)/shard_map/ppermute | solution.py:19
  146.3 1.9 collective-permute-start.3
  148.3 9.0 %all_gather.3 = f32[1,8,3,128]{3,0,2,1:T(1,128)S(1)} all-gather(f32[1,2,3,128]{3,0,2,1:T(1,128)S(1)} %copy.126), channel_id=1, replica_groups=mesh['box'=128,'coarse'=4] {'coarse'}, dimensions={1}, use_global_device_ids=true | all-gather | bytes 15360 | tf_op jit(solution)/shard_map/all_gather | solution.py:117
  157.3 9.8 %collective-permute-start = (f32[1,8,3,128]{3,0,2,1:T(1,128)S(1)}, f32[1,8,3,128]{3,0,2,1:T(1,128)S(1)}, u32[]{:S(2)}, u32[]{:S(2)}) collective-permute-start(f32[1,8,3,128]{3,0,2,1:T(1,128)S(1)} %all_gather.3), channel_id=1, source_target_pairs={{0,4},{4,8},{8,12},{12,16},{16,20},{20,24},{24,28},{28,32},{32,36}... | collective-permute-start | bytes 36872 | tf_op jit(solution)/shard_map/ppermute | solution.py:19
  167.2 2.1 collective-permute-start.1
  169.6 0.6 fusion.43
  170.4 7.0 %collective-permute-done.1 = f32[1,8,3,128]{3,0,2,1:T(1,128)S(1)} collective-permute-done((f32[1,8,3,128]{3,0,2,1:T(1,128)S(1)}, f32[1,8,3,128]{3,0,2,1:T(1,128)S(1)}, u32[]{:S(2)}, u32[]{:S(2)}) %collective-permute-start.1) | collective-permute-done | bytes 12320 | tf_op jit(solution)/shard_map/ppermute | solution.py:19
  177.4 1.1 multiply_reduce_fusion
  178.6 7.3 %fusion.13 = f32[2,128,512]{2,1,0:T(8,128)S(1)} fusion(f32[1,8,128,512]{3,2,1,0:T(8,128)S(1)} %collective-permute-done.3, f32[1,8,128,512]{3,2,1,0:T(8,128)} %bitcast.44, f32[1,8,128,512]{3,2,1,0:T(8,128)S(1)} %collective-permute-done.2, f32[2,24,128,128]{3,2,1,0:T(8,128)S(1)} %multiply_reduce_fusion, f32[2,24]{1,0:T(2,128)S(1)} %maximum_bitcast_fusion.7), kind=kOutput, calls=%fused_computation.24 | convolution fusion | flops 4836687872 | bytes 9961664 | tf_op jit(solution)/shard_map/vmap(bckl,cln->bkn)/dot_general | solution.py:85
  185.8 0.6 fusion.35
  186.5 0.6 fusion.20
  187.1 0.6 convolution_bitcast_fusion.1
  187.7 0.6 fusion.21
  188.3 0.6 fusion.22
  189.1 26.0 %scatter_fusion = f32[2,256,512]{2,1,0:T(8,128)S(1)} fusion(f32[2,256,512]{2,1,0:T(8,128)S(1)} %broadcast.682, s32[512]{0:T(512)S(1)} %bitcast.208, f32[512,512]{1,0:T(8,128)S(1)} %bitcast.209), kind=kCustom, calls=%fused_computation.3 | custom fusion | bytes 3149824 | tf_op jit(solution)/shard_map/vmap(vmap())/scatter | solution.py:100
  215.1 1.0 copy-done.2
  (79 shorter events, 6.2 us)
Async XLA Ops:
  0.0 101.7 %copy-start = (f32[1,2,256,512]{3,2,1,0:T(8,128)S(1)}, f32[1,2,256,512]{3,2,1,0:T(8,128)}, u32[]{:S(2)}) copy-start(f32[1,2,256,512]{3,2,1,0:T(8,128)} %param.14) | copy-start | bytes 3145732
  0.0 11.8 %copy-start.6 = (s32[1,2,256]{2,1,0:T(2,128)S(1)}, s32[1,2,256]{2,1,0:T(2,128)}, u32[]{:S(2)}) copy-start(s32[1,2,256]{2,1,0:T(2,128)} %param.11) | copy-start | bytes 6148
  0.0 7.1 %copy-start.1 = (f32[1,2,256]{2,1,0:T(2,128)S(1)}, f32[1,2,256]{2,1,0:T(2,128)}, u32[]{:S(2)}) copy-start(f32[1,2,256]{2,1,0:T(2,128)} %param.10) | copy-start | bytes 6148
  2.7 9.3 %copy-start.3 = (f32[1,2,128,128]{3,2,1,0:T(8,128)S(1)}, f32[1,2,128,128]{3,2,1,0:T(8,128)}, u32[]{:S(2)}) copy-start(f32[1,2,128,128]{3,2,1,0:T(8,128)} %param.12) | copy-start | bytes 393220
  57.6 24.4 %copy-start.4 = (f32[2,128,128]{2,1,0:T(8,128)}, f32[2,128,128]{2,1,0:T(8,128)S(1)}, u32[]{:S(2)}) copy-start(f32[2,128,128]{2,1,0:T(8,128)S(1)} %fusion.45) | copy-start | bytes 393220
  106.0 0.9 copy-start.5
  108.7 60.7 %copy-start.7 = (s32[1,2,6]{2,1,0:T(2,128)S(1)}, s32[1,2,6]{2,1,0:T(2,128)}, u32[]{:S(2)}) copy-start(s32[1,2,6]{2,1,0:T(2,128)} %param.13) | copy-start | bytes 148
  110.3 30.3 %all-to-all-start = ((f32[4,1,2,128,512]{4,3,2,1,0:T(8,128)}), f32[4,1,2,128,512]{4,3,2,1,0:T(8,128)}, u32[]{:S(2)}, u32[]{:S(2)}) async-start(f32[4,1,2,128,512]{4,3,2,1,0:T(8,128)} %stack.5), calls=%async_computation | async-start | bytes 4194304 | tf_op jit(solution)/shard_map/all_to_all | solution.py:13
  140.5 38.0 %collective-permute-start.2 = (f32[1,8,128,512]{3,2,1,0:T(8,128)}, f32[1,8,128,512]{3,2,1,0:T(8,128)S(1)}, u32[]{:S(2)}, u32[]{:S(2)}) collective-permute-start(f32[1,8,128,512]{3,2,1,0:T(8,128)} %bitcast.44), channel_id=1, source_target_pairs={{0,4},{4,8},{8,12},{12,16},{16,20},{20,24},{24,28},{28,32},{32,36}... | collective-permute-start | bytes 6291464 | tf_op jit(solution)/shard_map/ppermute | solution.py:19
  146.3 32.2 %collective-permute-start.3 = (f32[1,8,128,512]{3,2,1,0:T(8,128)}, f32[1,8,128,512]{3,2,1,0:T(8,128)S(1)}, u32[]{:S(2)}, u32[]{:S(2)}) collective-permute-start(f32[1,8,128,512]{3,2,1,0:T(8,128)} %bitcast.44), channel_id=1, source_target_pairs={{4,0},{8,4},{12,8},{16,12},{20,16},{24,20},{28,24},{32,28},{36,32}... | collective-permute-start | bytes 6291464 | tf_op jit(solution)/shard_map/ppermute | solution.py:19
  157.3 13.0 %collective-permute-start = (f32[1,8,3,128]{3,0,2,1:T(1,128)S(1)}, f32[1,8,3,128]{3,0,2,1:T(1,128)S(1)}, u32[]{:S(2)}, u32[]{:S(2)}) collective-permute-start(f32[1,8,3,128]{3,0,2,1:T(1,128)S(1)} %all_gather.3), channel_id=1, source_target_pairs={{0,4},{4,8},{8,12},{12,16},{16,20},{20,24},{24,28},{28,32},{32,36}... | collective-permute-start | bytes 36872 | tf_op jit(solution)/shard_map/ppermute | solution.py:19
  167.2 10.2 %collective-permute-start.1 = (f32[1,8,3,128]{3,0,2,1:T(1,128)S(1)}, f32[1,8,3,128]{3,0,2,1:T(1,128)S(1)}, u32[]{:S(2)}, u32[]{:S(2)}) collective-permute-start(f32[1,8,3,128]{3,0,2,1:T(1,128)S(1)} %all_gather.3), channel_id=1, source_target_pairs={{4,0},{8,4},{12,8},{16,12},{20,16},{24,20},{28,24},{32,28},{36,32}... | collective-permute-start | bytes 36872 | tf_op jit(solution)/shard_map/ppermute | solution.py:19
  215.1 1.0 copy-start.2
